TPU v7x, 512 devices: a whole 4x8x8 slice. The times are simulated.
512 devices in a mesh: span: 16 (over z_hi, x), wall: 16 (over y, core), stream: 2 (over z_lo).
Axes of the slice: x: 4, y: 8, z: 8 (z_hi: 4, z_lo: 2; z = z_hi * 2 + z_lo), core: 2. Of those that a mesh axis runs over, the one named last changes fastest.
Arguments:
- fields: float32 [4, 16, 256, 2048], P(None, 'stream', 'wall', 'span'), may hold values from -67.5 to 67.5, as said below
Outputs:
- clark_model: float32 [3, 16, 256, 2048], P(None, 'stream', 'wall', 'span')
- similar_model: float32 [3, 16, 256, 2048], P(None, 'stream', 'wall', 'span')
- clark_corr: float32 [3, 256], P(None, 'wall')
- similar_corr: float32 [3, 256], P(None, 'wall')
Inputs may be any that keep to these rules, and one draw needn't show every extreme that they name: The fields are rough from cell to cell.
All inputs are finite; a program needn't handle non-finite values.
Results may differ from a plain program's by a relative error of at most 0.00024.
Values sent between devices are 32-bit elements; how exact they have to be, the bound alone decides.
A program may use at most 64 MiB of HBM per device.

v0:
```python
import math
import jax
import jax.numpy as jnp
from jax import lax
from jax.sharding import PartitionSpec as P

raw_taps = [math.exp(-((k - 8) ** 2) / 18.0) for k in range(17)]
filter_taps = [value / sum(raw_taps) for value in raw_taps]
clark_coef = 9.0
small_eps = 1e-06


def with_halo(cells, sides, width, closed):
    for axis, dim in sides:
        count = lax.axis_size(axis)
        ends = count if closed else count - 1
        head = lax.slice_in_dim(cells, 0, width, axis=dim)
        tail = lax.slice_in_dim(cells, cells.shape[dim] - width, cells.shape[dim], axis=dim)
        cells = jnp.concatenate(
            [
                lax.ppermute(tail, axis, [(i, (i + 1) % count) for i in range(ends)]),
                cells,
                lax.ppermute(head, axis, [((i + 1) % count, i) for i in range(ends)]),
            ],
            axis=dim,
        )
    return cells


def band_matrix(length):
    offset = (
        jnp.arange(length + 16, dtype=jnp.int32)[:, None]
        - jnp.arange(length, dtype=jnp.int32)[None, :]
    )
    matrix = jnp.zeros((length + 16, length), jnp.float32)
    for k in range(17):
        matrix = matrix + jnp.where(offset == k, filter_taps[k], 0.0).astype(jnp.float32)
    return matrix


def smooth(padded, direction, length):
    matrix = band_matrix(length)
    if direction == 3:
        return jnp.einsum("fswz,zk->fswk", padded, matrix, precision=lax.Precision.HIGHEST)
    if direction == 2:
        return jnp.einsum("fswz,wk->fskz", padded, matrix, precision=lax.Precision.HIGHEST)
    return jnp.einsum("fswz,sk->fkwz", padded, matrix, precision=lax.Precision.HIGHEST)


def with_products(quad):
    return jnp.concatenate([quad, quad[:3] * quad[3:4]], axis=0)


def filter_all(quad):
    stream_len, wall_len, span_len = (quad.shape[1], quad.shape[2], quad.shape[3])
    payload = with_products(quad)
    spanned = with_halo(payload, (("span", 3),), 8, True)
    extended = with_halo(spanned, (("wall", 2), ("stream", 1)), 8, False)
    kept = extended[:4]
    result = smooth(extended, 3, span_len)
    result = smooth(result, 2, wall_len)
    return (smooth(result, 1, stream_len), kept)


def clark_flux(means):
    padded = with_halo(means, (("span", 3),), 1, True)
    along_span = (padded[..., 2:] - padded[..., :-2]) * 0.5
    plane = with_halo(means, (("wall", 2), ("stream", 1)), 1, False)
    along_wall = (plane[:, 1:-1, 2:, :] - plane[:, 1:-1, :-2, :]) * 0.5
    along_stream = (plane[:, 2:, 1:-1, :] - plane[:, :-2, 1:-1, :]) * 0.5
    total = along_span[:3] * along_span[3:4] + along_wall[:3] * along_wall[3:4]
    total = total + along_stream[:3] * along_stream[3:4]
    return clark_coef * total


def shards(fields):
    first, unused_rim = filter_all(fields)
    means = first[:4]
    exact = first[4:] - means[:3] * means[3:4]
    second, mean_rim = filter_all(means)
    similar = second[4:] - second[:3] * second[3:4]
    clark = clark_flux(means)
    sums = (
        jnp.sum(exact * clark, axis=(1, 3)),
        jnp.sum(exact * similar, axis=(1, 3)),
        jnp.sum(exact * exact, axis=(1, 3)),
        jnp.sum(clark * clark, axis=(1, 3)),
        jnp.sum(similar * similar, axis=(1, 3)),
    )
    cross_c, cross_s, power_e, power_c, power_s = lax.psum(
        (sums[0], sums[1], sums[2], sums[3], sums[4]), ("span", "stream")
    )
    plane_cells = float(
        fields.shape[1] * fields.shape[3] * lax.axis_size("stream") * lax.axis_size("span")
    )
    cross_c = cross_c / plane_cells
    cross_s = cross_s / plane_cells
    power_e = power_e / plane_cells
    power_c = power_c / plane_cells
    power_s = power_s / plane_cells
    clark_corr = cross_c / jnp.sqrt((power_e + small_eps) * (power_c + small_eps))
    similar_corr = cross_s / jnp.sqrt((power_e + small_eps) * (power_s + small_eps))
    clark_model = clark / jnp.sqrt(power_c + small_eps)[:, None, :, None]
    similar_model = similar / jnp.sqrt(power_s + small_eps)[:, None, :, None]
    return (clark_model, similar_model, clark_corr, similar_corr)


def solution(mesh):
    return jax.shard_map(
        shards,
        mesh=mesh,
        in_specs=(P(None, "stream", "wall", "span"),),
        out_specs=(
            P(None, "stream", "wall", "span"),
            P(None, "stream", "wall", "span"),
            P(None, "wall"),
            P(None, "wall"),
        ),
        check_vma=False,
    )
```

profile of v0, /device:TPU:16, one launch (start us, length us, event | category | flops | bytes accessed | tf_op | source)
XLA Modules:
  0.0 371.7 jit_solution(2666519787292298506)
XLA Ops:
  3.7 13.1 %collective-permute-start.1 = (f32[7,8,16,8]{3,2,1,0:T(8,128)S(1)}, f32[7,8,16,8]{3,2,1,0:T(8,128)S(1)}, u32[]{:S(2)}, u32[]{:S(2)}) collective-permute-start(f32[7,8,16,8]{3,2,1,0:T(8,128)S(1)} %get-tuple-element.31), channel_id=1, source_target_pairs={{32,0},{64,32},{96,64},{128,96},{160,128},{192,160},{224,192},{256... | collective-permute-start | bytes 86024 | tf_op jit(solution)/shard_map/ppermute | solution.py:23
  16.9 1.9 collective-permute-start
  18.8 17.7 %collective-permute-done.1 = f32[7,8,16,8]{3,2,1,0:T(8,128)S(1)} collective-permute-done((f32[7,8,16,8]{3,2,1,0:T(8,128)S(1)}, f32[7,8,16,8]{3,2,1,0:T(8,128)S(1)}, u32[]{:S(2)}, u32[]{:S(2)}) %collective-permute-start.1) | collective-permute-done | bytes 28704 | tf_op jit(solution)/shard_map/ppermute | solution.py:23
  36.4 8.3 %collective-permute-done = f32[7,8,16,8]{3,2,1,0:T(8,128)S(1)} collective-permute-done((f32[7,8,16,8]{3,2,1,0:T(8,128)S(1)}, f32[7,8,16,8]{3,2,1,0:T(8,128)S(1)}, u32[]{:S(2)}, u32[]{:S(2)}) %collective-permute-start) | collective-permute-done | bytes 28704 | tf_op jit(solution)/shard_map/ppermute | solution.py:21
  46.3 1.9 collective-permute-start.3
  48.2 2.4 collective-permute-start.2
  50.6 3.6 collective-permute-done.3
  54.2 3.8 %collective-permute-done.2 = f32[7,8,8,144]{3,2,1,0:T(8,128)S(1)} collective-permute-done((f32[7,8,8,144]{3,2,1,0:T(8,128)S(1)}, f32[7,8,8,144]{3,2,1,0:T(8,128)S(1)}, u32[]{:S(2)}, u32[]{:S(2)}) %collective-permute-start.2) | collective-permute-done | bytes 258080 | tf_op jit(solution)/shard_map/ppermute | solution.py:21
  59.8 4.8 %collective-permute-start.4 = (f32[7,8,32,144]{3,2,1,0:T(8,128)S(1)}, f32[7,8,32,144]{3,2,1,0:T(8,128)S(1)}, u32[]{:S(2)}, u32[]{:S(2)}) collective-permute-start(f32[7,8,32,144]{3,2,1,0:T(8,128)S(1)} %pad_maximum_fusion.1), channel_id=1, source_target_pairs={{0,1},{2,3},{4,5},{6,7},{8,9},{10,11},{12,13},{14,15},{16,17},{18,... | collective-permute-start | bytes 3096584 | tf_op jit(solution)/shard_map/ppermute | solution.py:21
  64.5 36.9 %collective-permute-done.5 = f32[7,8,32,144]{3,2,1,0:T(8,128)S(1)} collective-permute-done((f32[7,8,32,144]{3,2,1,0:T(8,128)S(1)}, f32[7,8,32,144]{3,2,1,0:T(8,128)S(1)}, u32[]{:S(2)}, u32[]{:S(2)}) %collective-permute-start.5) | collective-permute-done | bytes 1032224 | tf_op jit(solution)/shard_map/ppermute | solution.py:23
  102.8 4.7 %fusion = f32[7,24,32,128]{3,2,1,0:T(8,128)S(1)} fusion(f32[7,8,32,144]{3,2,1,0:T(8,128)S(1)} %collective-permute-done.5, f32[7,8,8,144]{3,2,1,0:T(8,128)S(1)} %collective-permute-done.3, f32[7,8,16,8]{3,2,1,0:T(8,128)S(1)} %collective-permute-done.1, f32[3,8,16,128]{3,2,1,0:T(8,128)S(1)} %slice_multiply_fusion.5, f32[4,8,16,128]{3,2,1,0:T(8,128)S(1)} %copy-done, ...), kind=kOutput, calls=%fused_computation | convolution fusion | flops 1195444224 | bytes 5849088 | tf_op jit(solution)/shard_map/fswz,zk->fswk/dot_general | solution.py:44
  107.5 1.5 fusion.61
  110.5 1.9 collective-permute-start.13
  112.4 3.9 %collective-permute-start.12 = (f32[7,8,16,8]{3,1,2,0:T(8,128)S(1)}, f32[7,8,16,8]{3,1,2,0:T(8,128)S(1)}, u32[]{:S(2)}, u32[]{:S(2)}) collective-permute-start(f32[7,8,16,8]{3,1,2,0:T(8,128)S(1)} %get-tuple-element.28), channel_id=1, source_target_pairs={{0,32},{32,64},{64,96},{96,128},{128,160},{160,192},{192,224},{224... | collective-permute-start | bytes 86024 | tf_op jit(solution)/shard_map/ppermute | solution.py:21
  116.3 14.1 %collective-permute-done.13 = f32[7,8,16,8]{3,1,2,0:T(8,128)S(1)} collective-permute-done((f32[7,8,16,8]{3,1,2,0:T(8,128)S(1)}, f32[7,8,16,8]{3,1,2,0:T(8,128)S(1)}, u32[]{:S(2)}, u32[]{:S(2)}) %collective-permute-start.13) | collective-permute-done | bytes 28704 | tf_op jit(solution)/shard_map/ppermute | solution.py:23
  130.4 8.3 %collective-permute-done.12 = f32[7,8,16,8]{3,1,2,0:T(8,128)S(1)} collective-permute-done((f32[7,8,16,8]{3,1,2,0:T(8,128)S(1)}, f32[7,8,16,8]{3,1,2,0:T(8,128)S(1)}, u32[]{:S(2)}, u32[]{:S(2)}) %collective-permute-start.12) | collective-permute-done | bytes 28704 | tf_op jit(solution)/shard_map/ppermute | solution.py:21
  139.3 1.9 collective-permute-start.15
  141.2 2.4 collective-permute-start.14
  143.6 3.6 collective-permute-done.15
  147.2 3.8 %collective-permute-done.14 = f32[7,8,8,144]{3,1,2,0:T(8,128)S(1)} collective-permute-done((f32[7,8,8,144]{3,1,2,0:T(8,128)S(1)}, f32[7,8,8,144]{3,1,2,0:T(8,128)S(1)}, u32[]{:S(2)}, u32[]{:S(2)}) %collective-permute-start.14) | collective-permute-done | bytes 258080 | tf_op jit(solution)/shard_map/ppermute | solution.py:21
  152.7 4.8 %collective-permute-start.16 = (f32[7,8,32,144]{3,1,2,0:T(8,128)S(1)}, f32[7,8,32,144]{3,1,2,0:T(8,128)S(1)}, u32[]{:S(2)}, u32[]{:S(2)}) collective-permute-start(f32[7,8,32,144]{3,1,2,0:T(8,128)S(1)} %pad_maximum_fusion.2), channel_id=1, source_target_pairs={{0,1},{2,3},{4,5},{6,7},{8,9},{10,11},{12,13},{14,15},{16,17},{18,... | collective-permute-start | bytes 3096584 | tf_op jit(solution)/shard_map/ppermute | solution.py:21
  157.5 3.3 collective-permute-start.9
  160.8 2.5 collective-permute-start.8
  163.3 3.1 collective-permute-done.8
  169.2 1.9 collective-permute-start.7
  171.2 38.2 %collective-permute-done.7 = f32[4,8,16,1]{3,1,2,0:T(8,128)S(1)} collective-permute-done((f32[4,8,16,1]{3,1,2,0:T(8,128)S(1)}, f32[4,8,16,1]{3,1,2,0:T(8,128)S(1)}, u32[]{:S(2)}, u32[]{:S(2)}) %collective-permute-start.7) | collective-permute-done | bytes 2080 | tf_op jit(solution)/shard_map/ppermute | solution.py:21
  209.3 1.9 collective-permute-start.6
  211.2 8.4 %collective-permute-done.6 = f32[4,8,16,1]{3,1,2,0:T(8,128)S(1)} collective-permute-done((f32[4,8,16,1]{3,1,2,0:T(8,128)S(1)}, f32[4,8,16,1]{3,1,2,0:T(8,128)S(1)}, u32[]{:S(2)}, u32[]{:S(2)}) %collective-permute-start.6) | collective-permute-done | bytes 2080 | tf_op jit(solution)/shard_map/ppermute | solution.py:23
  220.1 2.6 pad_maximum_fusion
  222.7 5.8 %fusion.16 = f32[7,24,32,128]{3,2,1,0:T(8,128)S(1)} fusion(f32[7,24,32,144]{3,1,2,0:T(8,128)S(1)} %pad_maximum_fusion), kind=kOutput, calls=%fused_computation.17 | convolution fusion | flops 1190025216 | bytes 5849088 | tf_op jit(solution)/shard_map/fswz,zk->fswk/dot_general | solution.py:44
  228.5 1.5 fusion.59
  231.8 137.7 %all-reduce = (f32[3,16]{1,0:T(4,128)S(1)}, f32[3,16]{1,0:T(4,128)S(1)}, f32[3,16]{1,0:T(4,128)S(1)}, f32[3,16]{1,0:T(4,128)S(1)}, f32[3,16]{1,0:T(4,128)S(1)}) all-reduce(f32[3,16]{1,0:T(4,128)S(1)} %get-tuple-element.11, f32[3,16]{1,0:T(4,128)S(1)} %get-tuple-element.12, ...), channel_id=1, replica_groups=mesh['span'=16,'wall'=16,'stream'=2] {'span','stream'}, use_global_device_ids=true, to_apply=%region_1.2 | all-reduce | flops 240 | bytes 1920 | tf_op jit(solution)/shard_map/psum | solution.py:90
  (40 shorter events, 18.4 us)
Async XLA Ops:
  2.4 55.6 %copy-start = (f32[4,8,16,128]{3,2,1,0:T(8,128)S(1)}, f32[4,8,16,128]{3,2,1,0:T(8,128)}, u32[]{:S(2)}) copy-start(f32[4,8,16,128]{3,2,1,0:T(8,128)} %param.1) | copy-start | bytes 786436
  3.7 32.7 %collective-permute-start.1 = (f32[7,8,16,8]{3,2,1,0:T(8,128)S(1)}, f32[7,8,16,8]{3,2,1,0:T(8,128)S(1)}, u32[]{:S(2)}, u32[]{:S(2)}) collective-permute-start(f32[7,8,16,8]{3,2,1,0:T(8,128)S(1)} %get-tuple-element.31), channel_id=1, source_target_pairs={{32,0},{64,32},{96,64},{128,96},{160,128},{192,160},{224,192},{256... | collective-permute-start | bytes 86024 | tf_op jit(solution)/shard_map/ppermute | solution.py:23
  16.9 27.9 %collective-permute-start = (f32[7,8,16,8]{3,2,1,0:T(8,128)S(1)}, f32[7,8,16,8]{3,2,1,0:T(8,128)S(1)}, u32[]{:S(2)}, u32[]{:S(2)}) collective-permute-start(f32[7,8,16,8]{3,2,1,0:T(8,128)S(1)} %get-tuple-element.30), channel_id=1, source_target_pairs={{0,32},{32,64},{64,96},{96,128},{128,160},{160,192},{192,224},{224... | collective-permute-start | bytes 86024 | tf_op jit(solution)/shard_map/ppermute | solution.py:21
  46.3 7.9 %collective-permute-start.3 = (f32[7,8,8,144]{3,2,1,0:T(8,128)S(1)}, f32[7,8,8,144]{3,2,1,0:T(8,128)S(1)}, u32[]{:S(2)}, u32[]{:S(2)}) collective-permute-start(f32[7,8,8,144]{3,2,1,0:T(8,128)S(1)} %get-tuple-element.23), channel_id=1, source_target_pairs={{2,0},{4,2},{6,4},{8,6},{10,8},{12,10},{14,12},{16,14},{18,16},{20... | collective-permute-start | bytes 774152 | tf_op jit(solution)/shard_map/ppermute | solution.py:23
  48.2 9.8 %collective-permute-start.2 = (f32[7,8,8,144]{3,2,1,0:T(8,128)S(1)}, f32[7,8,8,144]{3,2,1,0:T(8,128)S(1)}, u32[]{:S(2)}, u32[]{:S(2)}) collective-permute-start(f32[7,8,8,144]{3,2,1,0:T(8,128)S(1)} %get-tuple-element.22), channel_id=1, source_target_pairs={{0,2},{2,4},{4,6},{6,8},{8,10},{10,12},{12,14},{14,16},{16,18},{18... | collective-permute-start | bytes 774152 | tf_op jit(solution)/shard_map/ppermute | solution.py:21
  58.5 43.0 %collective-permute-start.5 = (f32[7,8,32,144]{3,2,1,0:T(8,128)S(1)}, f32[7,8,32,144]{3,2,1,0:T(8,128)S(1)}, u32[]{:S(2)}, u32[]{:S(2)}) collective-permute-start(f32[7,8,32,144]{3,2,1,0:T(8,128)S(1)} %pad_maximum_fusion.1), channel_id=1, source_target_pairs={{1,0},{3,2},{5,4},{7,6},{9,8},{11,10},{13,12},{15,14},{17,16},{19,... | collective-permute-start | bytes 3096584 | tf_op jit(solution)/shard_map/ppermute | solution.py:23
  59.8 43.0 %collective-permute-start.4 = (f32[7,8,32,144]{3,2,1,0:T(8,128)S(1)}, f32[7,8,32,144]{3,2,1,0:T(8,128)S(1)}, u32[]{:S(2)}, u32[]{:S(2)}) collective-permute-start(f32[7,8,32,144]{3,2,1,0:T(8,128)S(1)} %pad_maximum_fusion.1), channel_id=1, source_target_pairs={{0,1},{2,3},{4,5},{6,7},{8,9},{10,11},{12,13},{14,15},{16,17},{18,... | collective-permute-start | bytes 3096584 | tf_op jit(solution)/shard_map/ppermute | solution.py:21
  110.5 20.0 %collective-permute-start.13 = (f32[7,8,16,8]{3,1,2,0:T(8,128)S(1)}, f32[7,8,16,8]{3,1,2,0:T(8,128)S(1)}, u32[]{:S(2)}, u32[]{:S(2)}) collective-permute-start(f32[7,8,16,8]{3,1,2,0:T(8,128)S(1)} %get-tuple-element.29), channel_id=1, source_target_pairs={{32,0},{64,32},{96,64},{128,96},{160,128},{192,160},{224,192},{256... | collective-permute-start | bytes 86024 | tf_op jit(solution)/shard_map/ppermute | solution.py:23
  112.4 26.4 %collective-permute-start.12 = (f32[7,8,16,8]{3,1,2,0:T(8,128)S(1)}, f32[7,8,16,8]{3,1,2,0:T(8,128)S(1)}, u32[]{:S(2)}, u32[]{:S(2)}) collective-permute-start(f32[7,8,16,8]{3,1,2,0:T(8,128)S(1)} %get-tuple-element.28), channel_id=1, source_target_pairs={{0,32},{32,64},{64,96},{96,128},{128,160},{160,192},{192,224},{224... | collective-permute-start | bytes 86024 | tf_op jit(solution)/shard_map/ppermute | solution.py:21
  139.3 7.9 %collective-permute-start.15 = (f32[7,8,8,144]{3,1,2,0:T(8,128)S(1)}, f32[7,8,8,144]{3,1,2,0:T(8,128)S(1)}, u32[]{:S(2)}, u32[]{:S(2)}) collective-permute-start(f32[7,8,8,144]{3,1,2,0:T(8,128)S(1)} %get-tuple-element.21), channel_id=1, source_target_pairs={{2,0},{4,2},{6,4},{8,6},{10,8},{12,10},{14,12},{16,14},{18,16},{20... | collective-permute-start | bytes 774152 | tf_op jit(solution)/shard_map/ppermute | solution.py:23
  141.2 9.8 %collective-permute-start.14 = (f32[7,8,8,144]{3,1,2,0:T(8,128)S(1)}, f32[7,8,8,144]{3,1,2,0:T(8,128)S(1)}, u32[]{:S(2)}, u32[]{:S(2)}) collective-permute-start(f32[7,8,8,144]{3,1,2,0:T(8,128)S(1)} %get-tuple-element.20), channel_id=1, source_target_pairs={{0,2},{2,4},{4,6},{6,8},{8,10},{10,12},{12,14},{14,16},{16,18},{18... | collective-permute-start | bytes 774152 | tf_op jit(solution)/shard_map/ppermute | solution.py:21
  151.4 68.6 %collective-permute-start.17 = (f32[7,8,32,144]{3,1,2,0:T(8,128)S(1)}, f32[7,8,32,144]{3,1,2,0:T(8,128)S(1)}, u32[]{:S(2)}, u32[]{:S(2)}) collective-permute-start(f32[7,8,32,144]{3,1,2,0:T(8,128)S(1)} %pad_maximum_fusion.2), channel_id=1, source_target_pairs={{1,0},{3,2},{5,4},{7,6},{9,8},{11,10},{13,12},{15,14},{17,16},{19,... | collective-permute-start | bytes 3096584 | tf_op jit(solution)/shard_map/ppermute | solution.py:23
  152.7 67.3 %collective-permute-start.16 = (f32[7,8,32,144]{3,1,2,0:T(8,128)S(1)}, f32[7,8,32,144]{3,1,2,0:T(8,128)S(1)}, u32[]{:S(2)}, u32[]{:S(2)}) collective-permute-start(f32[7,8,32,144]{3,1,2,0:T(8,128)S(1)} %pad_maximum_fusion.2), channel_id=1, source_target_pairs={{0,1},{2,3},{4,5},{6,7},{8,9},{10,11},{12,13},{14,15},{16,17},{18,... | collective-permute-start | bytes 3096584 | tf_op jit(solution)/shard_map/ppermute | solution.py:21
  157.5 5.8 %collective-permute-start.9 = (f32[4,8,1,128]{3,1,2,0:T(8,128)S(1)}, f32[4,8,1,128]{3,1,2,0:T(8,128)S(1)}, u32[]{:S(2)}, u32[]{:S(2)}) collective-permute-start(f32[4,8,1,128]{3,1,2,0:T(8,128)S(1)} %get-tuple-element.26), channel_id=1, source_target_pairs={{0,2},{2,4},{4,6},{6,8},{8,10},{10,12},{12,14},{14,16},{16,18},{18... | collective-permute-start | bytes 49160 | tf_op jit(solution)/shard_map/ppermute | solution.py:21
  160.8 5.6 %collective-permute-start.8 = (f32[4,8,1,128]{3,1,2,0:T(8,128)S(1)}, f32[4,8,1,128]{3,1,2,0:T(8,128)S(1)}, u32[]{:S(2)}, u32[]{:S(2)}) collective-permute-start(f32[4,8,1,128]{3,1,2,0:T(8,128)S(1)} %get-tuple-element.27), channel_id=1, source_target_pairs={{2,0},{4,2},{6,4},{8,6},{10,8},{12,10},{14,12},{16,14},{18,16},{20... | collective-permute-start | bytes 49160 | tf_op jit(solution)/shard_map/ppermute | solution.py:23
  166.5 53.2 %collective-permute-start.11 = (f32[4,1,18,128]{3,1,2,0:T(1,128)S(1)}, f32[4,1,18,128]{3,1,2,0:T(1,128)S(1)}, u32[]{:S(2)}, u32[]{:S(2)}) collective-permute-start(f32[4,1,18,128]{3,1,2,0:T(1,128)S(1)} %get-tuple-element.35), channel_id=1, source_target_pairs={{0,1},{2,3},{4,5},{6,7},{8,9},{10,11},{12,13},{14,15},{16,17},{18,... | collective-permute-start | bytes 110600 | tf_op jit(solution)/shard_map/ppermute | solution.py:21
  167.8 51.9 %collective-permute-start.10 = (f32[4,1,18,128]{3,1,2,0:T(1,128)S(1)}, f32[4,1,18,128]{3,1,2,0:T(1,128)S(1)}, u32[]{:S(2)}, u32[]{:S(2)}) collective-permute-start(f32[4,1,18,128]{3,1,2,0:T(1,128)S(1)} %get-tuple-element.34), channel_id=1, source_target_pairs={{1,0},{3,2},{5,4},{7,6},{9,8},{11,10},{13,12},{15,14},{17,16},{19,... | collective-permute-start | bytes 110600 | tf_op jit(solution)/shard_map/ppermute | solution.py:23
  169.2 40.1 %collective-permute-start.7 = (f32[4,8,16,1]{3,1,2,0:T(8,128)S(1)}, f32[4,8,16,1]{3,1,2,0:T(8,128)S(1)}, u32[]{:S(2)}, u32[]{:S(2)}) collective-permute-start(f32[4,8,16,1]{3,1,2,0:T(8,128)S(1)} %get-tuple-element.25), channel_id=1, source_target_pairs={{0,32},{32,64},{64,96},{96,128},{128,160},{160,192},{192,224},{224... | collective-permute-start | bytes 6152 | tf_op jit(solution)/shard_map/ppermute | solution.py:21
  209.3 10.3 %collective-permute-start.6 = (f32[4,8,16,1]{3,1,2,0:T(8,128)S(1)}, f32[4,8,16,1]{3,1,2,0:T(8,128)S(1)}, u32[]{:S(2)}, u32[]{:S(2)}) collective-permute-start(f32[4,8,16,1]{3,1,2,0:T(8,128)S(1)} %get-tuple-element.24), channel_id=1, source_target_pairs={{32,0},{64,32},{96,64},{128,96},{160,128},{192,160},{224,192},{256... | collective-permute-start | bytes 6152 | tf_op jit(solution)/shard_map/ppermute | solution.py:23
where the time goes:
time: 372 us
  waiting for transfers between devices  151 us (41%)
  blocking collectives  138 us (37%)
  starting transfers between devices  53.8 us (14%)
  matrix products  15.9 us (4%)
  other arithmetic  9.48 us (3%)
    psum x1, blocking collectives, shards(): lax.psum((sums[0], sums[1], sums[2], sums[3], sums[4]), ('span', 'stream'))  138 us
    ppermute x9, waiting for transfers between devices, with_halo(): lax.ppermute(head, axis, [((i + 1) % count, i) for i in range(ends)])  87.4 us
    ppermute x9, waiting for transfers between devices, with_halo(): lax.ppermute(tail, axis, [(i, (i + 1) % count) for i in range(ends)])  63.8 us
    ppermute x9, starting transfers between devices, with_halo(): lax.ppermute(head, axis, [((i + 1) % count, i) for i in range(ends)])  27.1 us
    ppermute x9, starting transfers between devices, with_halo(): lax.ppermute(tail, axis, [(i, (i + 1) % count) for i in range(ends)])  26.7 us
    dot_general x2, matrix products, smooth(): jnp.einsum('fswz,zk->fswk', padded, matrix, precision=lax.Precision.HIGHEST)  10.5 us
  transfers between devices with their start and end apart: 18, of which 13 were waited for; matrix products, arithmetic and copies ran while one was open for 0% of the time, Pallas kernels for 0%

commit v1 on v0

--- a/solution.py
+++ b/solution.py
@@ -3,6 +3,7 @@
 import jax.numpy as jnp
 from jax import lax
 from jax.sharding import PartitionSpec as P
+from jax.lax import psum
 
 raw_taps = [math.exp(-((k - 8) ** 2) / 18.0) for k in range(17)]
 filter_taps = [value / sum(raw_taps) for value in raw_taps]
@@ -87,8 +88,8 @@
         jnp.sum(clark * clark, axis=(1, 3)),
         jnp.sum(similar * similar, axis=(1, 3)),
     )
-    cross_c, cross_s, power_e, power_c, power_s = lax.psum(
-        (sums[0], sums[1], sums[2], sums[3], sums[4]), ("span", "stream")
+    cross_c, cross_s, power_e, power_c, power_s = psum(
+        psum((sums[0], sums[1], sums[2], sums[3], sums[4]), "stream"), "span"
     )
     plane_cells = float(
         fields.shape[1] * fields.shape[3] * lax.axis_size("stream") * lax.axis_size("span")

time: 372 us -> 323 us (0.87)
  blocking collectives: 138 us -> 87.8 us
    psum x1 -> x2, blocking collectives: 138 us -> 87.8 us  [the longest x1 81.1 us: shards(): psum(psum((sums[0], sums[1], sums[2], sums[3], sums[4]), 'stream'), 'span')]
where the time goes in v1:
time: 323 us; the launch traced here: 322 us
  waiting for transfers between devices  151 us (47%)
  blocking collectives  87.8 us (27%)
  starting transfers between devices  53.8 us (17%)
  matrix products  15.9 us (5%)
  other arithmetic  9.48 us (3%)
    ppermute x9, waiting for transfers between devices, with_halo(): lax.ppermute(head, axis, [((i + 1) % count, i) for i in range(ends)])  87.4 us
    psum x1, blocking collectives, shards(): psum(psum((sums[0], sums[1], sums[2], sums[3], sums[4]), 'stream'), 'span')  81.1 us
    ppermute x9, waiting for transfers between devices, with_halo(): lax.ppermute(tail, axis, [(i, (i + 1) % count) for i in range(ends)])  63.8 us
    ppermute x9, starting transfers between devices, with_halo(): lax.ppermute(head, axis, [((i + 1) % count, i) for i in range(ends)])  27.1 us
    ppermute x9, starting transfers between devices, with_halo(): lax.ppermute(tail, axis, [(i, (i + 1) % count) for i in range(ends)])  26.7 us
    dot_general x2, matrix products, smooth(): jnp.einsum('fswz,zk->fswk', padded, matrix, precision=lax.Precision.HIGHEST)  10.5 us
    psum x1, blocking collectives, shards(): psum((sums[0], sums[1], sums[2], sums[3], sums[4]), 'stream')  6.7 us
  transfers between devices with their start and end apart: 18, of which 13 were waited for; matrix products, arithmetic and copies ran while one was open for 0% of the time, Pallas kernels for 0%

profile of v1, /device:TPU:16, one launch (start us, length us, event | category | flops | bytes accessed | tf_op | source)
XLA Modules:
  0.0 321.9 jit_solution(14738474464237699832)
XLA Ops:
  3.7 13.1 %collective-permute-start.1 = (f32[7,8,16,8]{3,2,1,0:T(8,128)S(1)}, f32[7,8,16,8]{3,2,1,0:T(8,128)S(1)}, u32[]{:S(2)}, u32[]{:S(2)}) collective-permute-start(f32[7,8,16,8]{3,2,1,0:T(8,128)S(1)} %get-tuple-element.36), channel_id=1, source_target_pairs={{32,0},{64,32},{96,64},{128,96},{160,128},{192,160},{224,192},{256... | collective-permute-start | bytes 86024 | tf_op jit(solution)/shard_map/ppermute | solution.py:24
  16.9 1.9 collective-permute-start
  18.8 17.7 %collective-permute-done.1 = f32[7,8,16,8]{3,2,1,0:T(8,128)S(1)} collective-permute-done((f32[7,8,16,8]{3,2,1,0:T(8,128)S(1)}, f32[7,8,16,8]{3,2,1,0:T(8,128)S(1)}, u32[]{:S(2)}, u32[]{:S(2)}) %collective-permute-start.1) | collective-permute-done | bytes 28704 | tf_op jit(solution)/shard_map/ppermute | solution.py:24
  36.4 8.3 %collective-permute-done = f32[7,8,16,8]{3,2,1,0:T(8,128)S(1)} collective-permute-done((f32[7,8,16,8]{3,2,1,0:T(8,128)S(1)}, f32[7,8,16,8]{3,2,1,0:T(8,128)S(1)}, u32[]{:S(2)}, u32[]{:S(2)}) %collective-permute-start) | collective-permute-done | bytes 28704 | tf_op jit(solution)/shard_map/ppermute | solution.py:22
  46.3 1.9 collective-permute-start.3
  48.2 2.4 collective-permute-start.2
  50.6 3.6 %collective-permute-done.3 = f32[7,8,8,144]{3,2,1,0:T(8,128)S(1)} collective-permute-done((f32[7,8,8,144]{3,2,1,0:T(8,128)S(1)}, f32[7,8,8,144]{3,2,1,0:T(8,128)S(1)}, u32[]{:S(2)}, u32[]{:S(2)}) %collective-permute-start.3) | collective-permute-done | bytes 258080 | tf_op jit(solution)/shard_map/ppermute | solution.py:24
  54.2 3.8 %collective-permute-done.2 = f32[7,8,8,144]{3,2,1,0:T(8,128)S(1)} collective-permute-done((f32[7,8,8,144]{3,2,1,0:T(8,128)S(1)}, f32[7,8,8,144]{3,2,1,0:T(8,128)S(1)}, u32[]{:S(2)}, u32[]{:S(2)}) %collective-permute-start.2) | collective-permute-done | bytes 258080 | tf_op jit(solution)/shard_map/ppermute | solution.py:22
  59.8 4.8 %collective-permute-start.4 = (f32[7,8,32,144]{3,2,1,0:T(8,128)S(1)}, f32[7,8,32,144]{3,2,1,0:T(8,128)S(1)}, u32[]{:S(2)}, u32[]{:S(2)}) collective-permute-start(f32[7,8,32,144]{3,2,1,0:T(8,128)S(1)} %pad_maximum_fusion.1), channel_id=1, source_target_pairs={{0,1},{2,3},{4,5},{6,7},{8,9},{10,11},{12,13},{14,15},{16,17},{18,... | collective-permute-start | bytes 3096584 | tf_op jit(solution)/shard_map/ppermute | solution.py:22
  64.5 36.9 %collective-permute-done.5 = f32[7,8,32,144]{3,2,1,0:T(8,128)S(1)} collective-permute-done((f32[7,8,32,144]{3,2,1,0:T(8,128)S(1)}, f32[7,8,32,144]{3,2,1,0:T(8,128)S(1)}, u32[]{:S(2)}, u32[]{:S(2)}) %collective-permute-start.5) | collective-permute-done | bytes 1032224 | tf_op jit(solution)/shard_map/ppermute | solution.py:24
  102.8 4.7 %fusion = f32[7,24,32,128]{3,2,1,0:T(8,128)S(1)} fusion(f32[7,8,32,144]{3,2,1,0:T(8,128)S(1)} %collective-permute-done.5, f32[7,8,8,144]{3,2,1,0:T(8,128)S(1)} %collective-permute-done.3, f32[7,8,16,8]{3,2,1,0:T(8,128)S(1)} %collective-permute-done.1, f32[3,8,16,128]{3,2,1,0:T(8,128)S(1)} %slice_multiply_fusion.5, f32[4,8,16,128]{3,2,1,0:T(8,128)S(1)} %copy-done, ...), kind=kOutput, calls=%fused_computation | convolution fusion | flops 1195444224 | bytes 5849088 | tf_op jit(solution)/shard_map/fswz,zk->fswk/dot_general | solution.py:45
  107.5 1.5 fusion.61
  110.5 1.9 collective-permute-start.13
  112.4 3.9 %collective-permute-start.12 = (f32[7,8,16,8]{3,1,2,0:T(8,128)S(1)}, f32[7,8,16,8]{3,1,2,0:T(8,128)S(1)}, u32[]{:S(2)}, u32[]{:S(2)}) collective-permute-start(f32[7,8,16,8]{3,1,2,0:T(8,128)S(1)} %get-tuple-element.33), channel_id=1, source_target_pairs={{0,32},{32,64},{64,96},{96,128},{128,160},{160,192},{192,224},{224... | collective-permute-start | bytes 86024 | tf_op jit(solution)/shard_map/ppermute | solution.py:22
  116.3 14.1 %collective-permute-done.13 = f32[7,8,16,8]{3,1,2,0:T(8,128)S(1)} collective-permute-done((f32[7,8,16,8]{3,1,2,0:T(8,128)S(1)}, f32[7,8,16,8]{3,1,2,0:T(8,128)S(1)}, u32[]{:S(2)}, u32[]{:S(2)}) %collective-permute-start.13) | collective-permute-done | bytes 28704 | tf_op jit(solution)/shard_map/ppermute | solution.py:24
  130.4 8.3 %collective-permute-done.12 = f32[7,8,16,8]{3,1,2,0:T(8,128)S(1)} collective-permute-done((f32[7,8,16,8]{3,1,2,0:T(8,128)S(1)}, f32[7,8,16,8]{3,1,2,0:T(8,128)S(1)}, u32[]{:S(2)}, u32[]{:S(2)}) %collective-permute-start.12) | collective-permute-done | bytes 28704 | tf_op jit(solution)/shard_map/ppermute | solution.py:22
  139.3 1.9 collective-permute-start.15
  141.2 2.4 collective-permute-start.14
  143.6 3.6 %collective-permute-done.15 = f32[7,8,8,144]{3,1,2,0:T(8,128)S(1)} collective-permute-done((f32[7,8,8,144]{3,1,2,0:T(8,128)S(1)}, f32[7,8,8,144]{3,1,2,0:T(8,128)S(1)}, u32[]{:S(2)}, u32[]{:S(2)}) %collective-permute-start.15) | collective-permute-done | bytes 258080 | tf_op jit(solution)/shard_map/ppermute | solution.py:24
  147.2 3.8 %collective-permute-done.14 = f32[7,8,8,144]{3,1,2,0:T(8,128)S(1)} collective-permute-done((f32[7,8,8,144]{3,1,2,0:T(8,128)S(1)}, f32[7,8,8,144]{3,1,2,0:T(8,128)S(1)}, u32[]{:S(2)}, u32[]{:S(2)}) %collective-permute-start.14) | collective-permute-done | bytes 258080 | tf_op jit(solution)/shard_map/ppermute | solution.py:22
  152.7 4.8 %collective-permute-start.16 = (f32[7,8,32,144]{3,1,2,0:T(8,128)S(1)}, f32[7,8,32,144]{3,1,2,0:T(8,128)S(1)}, u32[]{:S(2)}, u32[]{:S(2)}) collective-permute-start(f32[7,8,32,144]{3,1,2,0:T(8,128)S(1)} %pad_maximum_fusion.2), channel_id=1, source_target_pairs={{0,1},{2,3},{4,5},{6,7},{8,9},{10,11},{12,13},{14,15},{16,17},{18,... | collective-permute-start | bytes 3096584 | tf_op jit(solution)/shard_map/ppermute | solution.py:22
  157.5 3.3 %collective-permute-start.9 = (f32[4,8,1,128]{3,1,2,0:T(8,128)S(1)}, f32[4,8,1,128]{3,1,2,0:T(8,128)S(1)}, u32[]{:S(2)}, u32[]{:S(2)}) collective-permute-start(f32[4,8,1,128]{3,1,2,0:T(8,128)S(1)} %get-tuple-element.31), channel_id=1, source_target_pairs={{0,2},{2,4},{4,6},{6,8},{8,10},{10,12},{12,14},{14,16},{16,18},{18... | collective-permute-start | bytes 49160 | tf_op jit(solution)/shard_map/ppermute | solution.py:22
  160.8 2.5 collective-permute-start.8
  163.3 3.1 collective-permute-done.8
  169.2 1.9 collective-permute-start.7
  171.2 38.2 %collective-permute-done.7 = f32[4,8,16,1]{3,1,2,0:T(8,128)S(1)} collective-permute-done((f32[4,8,16,1]{3,1,2,0:T(8,128)S(1)}, f32[4,8,16,1]{3,1,2,0:T(8,128)S(1)}, u32[]{:S(2)}, u32[]{:S(2)}) %collective-permute-start.7) | collective-permute-done | bytes 2080 | tf_op jit(solution)/shard_map/ppermute | solution.py:22
  209.3 1.9 collective-permute-start.6
  211.2 8.4 %collective-permute-done.6 = f32[4,8,16,1]{3,1,2,0:T(8,128)S(1)} collective-permute-done((f32[4,8,16,1]{3,1,2,0:T(8,128)S(1)}, f32[4,8,16,1]{3,1,2,0:T(8,128)S(1)}, u32[]{:S(2)}, u32[]{:S(2)}) %collective-permute-start.6) | collective-permute-done | bytes 2080 | tf_op jit(solution)/shard_map/ppermute | solution.py:24
  220.1 2.6 pad_maximum_fusion
  222.7 5.8 %fusion.16 = f32[7,24,32,128]{3,2,1,0:T(8,128)S(1)} fusion(f32[7,24,32,144]{3,1,2,0:T(8,128)S(1)} %pad_maximum_fusion), kind=kOutput, calls=%fused_computation.17 | convolution fusion | flops 1190025216 | bytes 5849088 | tf_op jit(solution)/shard_map/fswz,zk->fswk/dot_general | solution.py:45
  231.8 6.7 %all-reduce.1 = (f32[3,16]{1,0:T(4,128)S(1)}, f32[3,16]{1,0:T(4,128)S(1)}, f32[3,16]{1,0:T(4,128)S(1)}, f32[3,16]{1,0:T(4,128)S(1)}, f32[3,16]{1,0:T(4,128)S(1)}) all-reduce(f32[3,16]{1,0:T(4,128)S(1)} %get-tuple-element.11, f32[3,16]{1,0:T(4,128)S(1)} %get-tuple-element.12, ...), channel_id=1, replica_groups=mesh['span'=16,'wall'=16,'stream'=2] {'stream'}, use_global_device_ids=true, to_apply=%region_1.2 | all-reduce | flops 240 | bytes 1920 | tf_op jit(solution)/shard_map/psum | solution.py:92
  238.5 81.1 %all-reduce = (f32[3,16]{1,0:T(4,128)S(1)}, f32[3,16]{1,0:T(4,128)S(1)}, f32[3,16]{1,0:T(4,128)S(1)}, f32[3,16]{1,0:T(4,128)S(1)}, f32[3,16]{1,0:T(4,128)S(1)}) all-reduce(f32[3,16]{1,0:T(4,128)S(1)} %get-tuple-element.18, f32[3,16]{1,0:T(4,128)S(1)} %get-tuple-element.19, ...), channel_id=1, replica_groups=mesh['span'=16,'wall'=16,'stream'=2] {'span'}, use_global_device_ids=true, to_apply=%region_2.3 | all-reduce | flops 240 | bytes 1920 | tf_op jit(solution)/shard_map/psum | solution.py:91
  (41 shorter events, 19.9 us)
Async XLA Ops:
  2.4 55.6 %copy-start = (f32[4,8,16,128]{3,2,1,0:T(8,128)S(1)}, f32[4,8,16,128]{3,2,1,0:T(8,128)}, u32[]{:S(2)}) copy-start(f32[4,8,16,128]{3,2,1,0:T(8,128)} %param.1) | copy-start | bytes 786436
  3.7 32.7 %collective-permute-start.1 = (f32[7,8,16,8]{3,2,1,0:T(8,128)S(1)}, f32[7,8,16,8]{3,2,1,0:T(8,128)S(1)}, u32[]{:S(2)}, u32[]{:S(2)}) collective-permute-start(f32[7,8,16,8]{3,2,1,0:T(8,128)S(1)} %get-tuple-element.36), channel_id=1, source_target_pairs={{32,0},{64,32},{96,64},{128,96},{160,128},{192,160},{224,192},{256... | collective-permute-start | bytes 86024 | tf_op jit(solution)/shard_map/ppermute | solution.py:24
  16.9 27.9 %collective-permute-start = (f32[7,8,16,8]{3,2,1,0:T(8,128)S(1)}, f32[7,8,16,8]{3,2,1,0:T(8,128)S(1)}, u32[]{:S(2)}, u32[]{:S(2)}) collective-permute-start(f32[7,8,16,8]{3,2,1,0:T(8,128)S(1)} %get-tuple-element.35), channel_id=1, source_target_pairs={{0,32},{32,64},{64,96},{96,128},{128,160},{160,192},{192,224},{224... | collective-permute-start | bytes 86024 | tf_op jit(solution)/shard_map/ppermute | solution.py:22
  46.3 7.9 %collective-permute-start.3 = (f32[7,8,8,144]{3,2,1,0:T(8,128)S(1)}, f32[7,8,8,144]{3,2,1,0:T(8,128)S(1)}, u32[]{:S(2)}, u32[]{:S(2)}) collective-permute-start(f32[7,8,8,144]{3,2,1,0:T(8,128)S(1)} %get-tuple-element.28), channel_id=1, source_target_pairs={{2,0},{4,2},{6,4},{8,6},{10,8},{12,10},{14,12},{16,14},{18,16},{20... | collective-permute-start | bytes 774152 | tf_op jit(solution)/shard_map/ppermute | solution.py:24
  48.2 9.8 %collective-permute-start.2 = (f32[7,8,8,144]{3,2,1,0:T(8,128)S(1)}, f32[7,8,8,144]{3,2,1,0:T(8,128)S(1)}, u32[]{:S(2)}, u32[]{:S(2)}) collective-permute-start(f32[7,8,8,144]{3,2,1,0:T(8,128)S(1)} %get-tuple-element.27), channel_id=1, source_target_pairs={{0,2},{2,4},{4,6},{6,8},{8,10},{10,12},{12,14},{14,16},{16,18},{18... | collective-permute-start | bytes 774152 | tf_op jit(solution)/shard_map/ppermute | solution.py:22
  58.5 43.0 %collective-permute-start.5 = (f32[7,8,32,144]{3,2,1,0:T(8,128)S(1)}, f32[7,8,32,144]{3,2,1,0:T(8,128)S(1)}, u32[]{:S(2)}, u32[]{:S(2)}) collective-permute-start(f32[7,8,32,144]{3,2,1,0:T(8,128)S(1)} %pad_maximum_fusion.1), channel_id=1, source_target_pairs={{1,0},{3,2},{5,4},{7,6},{9,8},{11,10},{13,12},{15,14},{17,16},{19,... | collective-permute-start | bytes 3096584 | tf_op jit(solution)/shard_map/ppermute | solution.py:24
  59.8 43.0 %collective-permute-start.4 = (f32[7,8,32,144]{3,2,1,0:T(8,128)S(1)}, f32[7,8,32,144]{3,2,1,0:T(8,128)S(1)}, u32[]{:S(2)}, u32[]{:S(2)}) collective-permute-start(f32[7,8,32,144]{3,2,1,0:T(8,128)S(1)} %pad_maximum_fusion.1), channel_id=1, source_target_pairs={{0,1},{2,3},{4,5},{6,7},{8,9},{10,11},{12,13},{14,15},{16,17},{18,... | collective-permute-start | bytes 3096584 | tf_op jit(solution)/shard_map/ppermute | solution.py:22
  110.5 20.0 %collective-permute-start.13 = (f32[7,8,16,8]{3,1,2,0:T(8,128)S(1)}, f32[7,8,16,8]{3,1,2,0:T(8,128)S(1)}, u32[]{:S(2)}, u32[]{:S(2)}) collective-permute-start(f32[7,8,16,8]{3,1,2,0:T(8,128)S(1)} %get-tuple-element.34), channel_id=1, source_target_pairs={{32,0},{64,32},{96,64},{128,96},{160,128},{192,160},{224,192},{256... | collective-permute-start | bytes 86024 | tf_op jit(solution)/shard_map/ppermute | solution.py:24
  112.4 26.4 %collective-permute-start.12 = (f32[7,8,16,8]{3,1,2,0:T(8,128)S(1)}, f32[7,8,16,8]{3,1,2,0:T(8,128)S(1)}, u32[]{:S(2)}, u32[]{:S(2)}) collective-permute-start(f32[7,8,16,8]{3,1,2,0:T(8,128)S(1)} %get-tuple-element.33), channel_id=1, source_target_pairs={{0,32},{32,64},{64,96},{96,128},{128,160},{160,192},{192,224},{224... | collective-permute-start | bytes 86024 | tf_op jit(solution)/shard_map/ppermute | solution.py:22
  139.3 7.9 %collective-permute-start.15 = (f32[7,8,8,144]{3,1,2,0:T(8,128)S(1)}, f32[7,8,8,144]{3,1,2,0:T(8,128)S(1)}, u32[]{:S(2)}, u32[]{:S(2)}) collective-permute-start(f32[7,8,8,144]{3,1,2,0:T(8,128)S(1)} %get-tuple-element.26), channel_id=1, source_target_pairs={{2,0},{4,2},{6,4},{8,6},{10,8},{12,10},{14,12},{16,14},{18,16},{20... | collective-permute-start | bytes 774152 | tf_op jit(solution)/shard_map/ppermute | solution.py:24
  141.2 9.8 %collective-permute-start.14 = (f32[7,8,8,144]{3,1,2,0:T(8,128)S(1)}, f32[7,8,8,144]{3,1,2,0:T(8,128)S(1)}, u32[]{:S(2)}, u32[]{:S(2)}) collective-permute-start(f32[7,8,8,144]{3,1,2,0:T(8,128)S(1)} %get-tuple-element.25), channel_id=1, source_target_pairs={{0,2},{2,4},{4,6},{6,8},{8,10},{10,12},{12,14},{14,16},{16,18},{18... | collective-permute-start | bytes 774152 | tf_op jit(solution)/shard_map/ppermute | solution.py:22
  151.4 68.6 %collective-permute-start.17 = (f32[7,8,32,144]{3,1,2,0:T(8,128)S(1)}, f32[7,8,32,144]{3,1,2,0:T(8,128)S(1)}, u32[]{:S(2)}, u32[]{:S(2)}) collective-permute-start(f32[7,8,32,144]{3,1,2,0:T(8,128)S(1)} %pad_maximum_fusion.2), channel_id=1, source_target_pairs={{1,0},{3,2},{5,4},{7,6},{9,8},{11,10},{13,12},{15,14},{17,16},{19,... | collective-permute-start | bytes 3096584 | tf_op jit(solution)/shard_map/ppermute | solution.py:24
  152.7 67.3 %collective-permute-start.16 = (f32[7,8,32,144]{3,1,2,0:T(8,128)S(1)}, f32[7,8,32,144]{3,1,2,0:T(8,128)S(1)}, u32[]{:S(2)}, u32[]{:S(2)}) collective-permute-start(f32[7,8,32,144]{3,1,2,0:T(8,128)S(1)} %pad_maximum_fusion.2), channel_id=1, source_target_pairs={{0,1},{2,3},{4,5},{6,7},{8,9},{10,11},{12,13},{14,15},{16,17},{18,... | collective-permute-start | bytes 3096584 | tf_op jit(solution)/shard_map/ppermute | solution.py:22
  157.5 5.8 %collective-permute-start.9 = (f32[4,8,1,128]{3,1,2,0:T(8,128)S(1)}, f32[4,8,1,128]{3,1,2,0:T(8,128)S(1)}, u32[]{:S(2)}, u32[]{:S(2)}) collective-permute-start(f32[4,8,1,128]{3,1,2,0:T(8,128)S(1)} %get-tuple-element.31), channel_id=1, source_target_pairs={{0,2},{2,4},{4,6},{6,8},{8,10},{10,12},{12,14},{14,16},{16,18},{18... | collective-permute-start | bytes 49160 | tf_op jit(solution)/shard_map/ppermute | solution.py:22
  160.8 5.6 %collective-permute-start.8 = (f32[4,8,1,128]{3,1,2,0:T(8,128)S(1)}, f32[4,8,1,128]{3,1,2,0:T(8,128)S(1)}, u32[]{:S(2)}, u32[]{:S(2)}) collective-permute-start(f32[4,8,1,128]{3,1,2,0:T(8,128)S(1)} %get-tuple-element.32), channel_id=1, source_target_pairs={{2,0},{4,2},{6,4},{8,6},{10,8},{12,10},{14,12},{16,14},{18,16},{20... | collective-permute-start | bytes 49160 | tf_op jit(solution)/shard_map/ppermute | solution.py:24
  166.5 53.2 %collective-permute-start.11 = (f32[4,1,18,128]{3,1,2,0:T(1,128)S(1)}, f32[4,1,18,128]{3,1,2,0:T(1,128)S(1)}, u32[]{:S(2)}, u32[]{:S(2)}) collective-permute-start(f32[4,1,18,128]{3,1,2,0:T(1,128)S(1)} %get-tuple-element.40), channel_id=1, source_target_pairs={{0,1},{2,3},{4,5},{6,7},{8,9},{10,11},{12,13},{14,15},{16,17},{18,... | collective-permute-start | bytes 110600 | tf_op jit(solution)/shard_map/ppermute | solution.py:22
  167.8 51.9 %collective-permute-start.10 = (f32[4,1,18,128]{3,1,2,0:T(1,128)S(1)}, f32[4,1,18,128]{3,1,2,0:T(1,128)S(1)}, u32[]{:S(2)}, u32[]{:S(2)}) collective-permute-start(f32[4,1,18,128]{3,1,2,0:T(1,128)S(1)} %get-tuple-element.39), channel_id=1, source_target_pairs={{1,0},{3,2},{5,4},{7,6},{9,8},{11,10},{13,12},{15,14},{17,16},{19,... | collective-permute-start | bytes 110600 | tf_op jit(solution)/shard_map/ppermute | solution.py:24
  169.2 40.1 %collective-permute-start.7 = (f32[4,8,16,1]{3,1,2,0:T(8,128)S(1)}, f32[4,8,16,1]{3,1,2,0:T(8,128)S(1)}, u32[]{:S(2)}, u32[]{:S(2)}) collective-permute-start(f32[4,8,16,1]{3,1,2,0:T(8,128)S(1)} %get-tuple-element.30), channel_id=1, source_target_pairs={{0,32},{32,64},{64,96},{96,128},{128,160},{160,192},{192,224},{224... | collective-permute-start | bytes 6152 | tf_op jit(solution)/shard_map/ppermute | solution.py:22
  209.3 10.3 %collective-permute-start.6 = (f32[4,8,16,1]{3,1,2,0:T(8,128)S(1)}, f32[4,8,16,1]{3,1,2,0:T(8,128)S(1)}, u32[]{:S(2)}, u32[]{:S(2)}) collective-permute-start(f32[4,8,16,1]{3,1,2,0:T(8,128)S(1)} %get-tuple-element.29), channel_id=1, source_target_pairs={{32,0},{64,32},{96,64},{128,96},{160,128},{192,160},{224,192},{256... | collective-permute-start | bytes 6152 | tf_op jit(solution)/shard_map/ppermute | solution.py:24
